TPU v7x, 32 devices: a whole 2x2x4 slice. The times are simulated.
32 devices in a mesh: dp: 2 (over core), shard: 16 (over z, y, x).
Axes of the slice: x: 2, y: 2, z: 4, core: 2. Of those that a mesh axis runs over, the one named last changes fastest.
Arguments:
- hidden_in: bfloat16 [4096, 1024], P(('dp', 'shard')), may hold values from -6 to 6
- doc_ids: int32 [32, 128], P(('dp', 'shard')), may hold values from 0 to 3, never falling along the last dimension, each value on 1 to 64 neighbouring positions
- expert_ids: int32 [4096], P(('dp', 'shard')), may hold values from 0 to 1, as said below
- slot_ids: int32 [4096], P(('dp', 'shard')), may hold values from 0 to 73, as said below
- out_grad: bfloat16 [4096, 1024], P(('dp', 'shard')), may hold values from -6 to 6
- ln1_gain: bfloat16 [1024], P(('dp', 'shard')), may hold values from 0.5 to 1.5
- ln1_bias: bfloat16 [1024], P(('dp', 'shard')), may hold values from -1 to 1
- w_query: bfloat16 [1024, 1024], P(('dp', 'shard')), may hold values from -0.1875 to 0.1875
- w_key: bfloat16 [1024, 1024], P(('dp', 'shard')), may hold values from -0.1875 to 0.1875
- w_value: bfloat16 [1024, 1024], P(('dp', 'shard')), may hold values from -0.1875 to 0.1875
- w_out: bfloat16 [1024, 1024], P(('dp', 'shard')), may hold values from -0.5 to 0.5
- ln2_gain: bfloat16 [1024], P(('dp', 'shard')), may hold values from 0.5 to 1.5
- ln2_bias: bfloat16 [1024], P(('dp', 'shard')), may hold values from -1 to 1
- w_up: bfloat16 [1024, 4096], P(('dp', 'shard')), may hold values from -0.1875 to 0.1875
- w_down: bfloat16 [4096, 1024], P(('dp', 'shard')), may hold values from -0.09375 to 0.09375
- w_router: bfloat16 [1024, 2], P(('dp', 'shard')), may hold values from -0.125 to 0.125
- w_mix: bfloat16 [1024, 2], P(('dp', 'shard')), may hold values from -0.1875 to 0.1875
- expert_up: bfloat16 [2, 1024, 4096], P(None, ('dp', 'shard')), may hold values from -0.1875 to 0.1875
- expert_down: bfloat16 [2, 4096, 1024], P(None, ('dp', 'shard')), may hold values from -0.09375 to 0.09375
- load_avg: float32 [2], replicated, may hold values from 0.05 to 0.3
Outputs:
- layer_out: bfloat16 [4096, 1024], P(('dp', 'shard'))
- input_grad: bfloat16 [4096, 1024], P(('dp', 'shard'))
- grad_ln1_gain: float32 [1024], P(('dp', 'shard'))
- grad_ln1_bias: float32 [1024], P(('dp', 'shard'))
- grad_w_query: float32 [1024, 1024], P(('dp', 'shard'))
- grad_w_key: float32 [1024, 1024], P(('dp', 'shard'))
- grad_w_value: float32 [1024, 1024], P(('dp', 'shard'))
- grad_w_out: float32 [1024, 1024], P(('dp', 'shard'))
- grad_ln2_gain: float32 [1024], P(('dp', 'shard'))
- grad_ln2_bias: float32 [1024], P(('dp', 'shard'))
- grad_w_up: float32 [1024, 4096], P(('dp', 'shard'))
- grad_w_down: float32 [4096, 1024], P(('dp', 'shard'))
- grad_w_router: float32 [1024, 2], P(('dp', 'shard'))
- grad_w_mix: float32 [1024, 2], P(('dp', 'shard'))
- grad_expert_up: float32 [2, 1024, 4096], P(None, ('dp', 'shard'))
- grad_expert_down: float32 [2, 4096, 1024], P(None, ('dp', 'shard'))
- expert_counts: int32 [2], replicated
- load_avg_new: float32 [2], replicated
Inputs may be any that keep to these rules, and one draw needn't show every extreme that they name: `expert_ids`: of the 128 tokens of one sequence at most 74 go to one expert, and in some sequence exactly 74 do. `slot_ids`: A token's slot is the number of earlier tokens of the same sequence routed to the same expert.
All inputs are finite; a program needn't handle non-finite values.
Results may differ from a plain program's by a relative error of at most 0.012.
The roundings to bfloat16 on the way count: a program that leaves them out, or rounds other values in their place, can miss the bound.
Values may be sent and summed in bfloat16 or wider, within the bound.
A program may use at most 384 MiB of HBM per device.

v0:
```python
import jax
import jax.numpy as jnp
from jax import lax
from jax.sharding import PartitionSpec as P

HEADS = 16
CAP = 74
BF = jnp.bfloat16
F32 = jnp.float32
BOTH = ("dp", "shard")


def mm(a, b, dims=((1,), (0,))):
    return lax.dot_general(a, b, (dims, ((), ())), preferred_element_type=F32)


def layer_norm(values, gain, bias):
    centre = values - jnp.mean(values, axis=-1, keepdims=True)
    scale_inv = lax.rsqrt(jnp.mean(centre * centre, axis=-1, keepdims=True) + 1e-05)
    normed = centre * scale_inv
    return (normed * gain + bias, normed, scale_inv)


def norm_back(grad_out, normed, scale_inv, gain):
    grad_normed = grad_out * gain
    inner = grad_normed - jnp.mean(grad_normed, axis=-1, keepdims=True)
    inner = inner - normed * jnp.mean(grad_normed * normed, axis=-1, keepdims=True)
    return (scale_inv * inner, jnp.sum(grad_out * normed, axis=0), jnp.sum(grad_out, axis=0))


def gelu_pair(t):
    inner = 0.7978845608 * (t + 0.044715 * t * t * t)
    th = jnp.tanh(inner)
    val = 0.5 * t * (1.0 + th)
    der = 0.5 * (1.0 + th) + 0.5 * t * (1.0 - th * th) * 0.7978845608 * (
        1.0 + 3.0 * 0.044715 * t * t
    )
    return (val, der)


def ag(block):
    return lax.all_gather(block, "shard", axis=0, tiled=False)


def rs(parts):
    return lax.psum_scatter(parts.astype(BF), "shard", scatter_dimension=0, tiled=False).astype(F32)


def body(
    hidden_in,
    doc_ids,
    expert_ids,
    slot_ids,
    out_grad,
    ln1_gain,
    ln1_bias,
    w_query,
    w_key,
    w_value,
    w_out,
    ln2_gain,
    ln2_bias,
    w_up,
    w_down,
    w_router,
    w_mix,
    expert_up,
    expert_down,
    load_avg,
):
    T, D = hidden_in.shape
    H, HD = (HEADS, D // HEADS)
    S = lax.axis_size("shard")
    C = lax.axis_size("dp")
    WR = w_query.shape[0]
    FF = w_up.shape[1]
    FR = w_down.shape[0]
    F = FR * C
    E = expert_up.shape[0]
    LO, HI = (80, T - 80)
    pos = jnp.where(
        expert_ids == 0, slot_ids, jnp.sum((expert_ids == 0).astype(jnp.int32)) + slot_ids
    )
    n0 = jnp.sum((expert_ids == 0).astype(jnp.int32))
    place = lax.iota(jnp.int32, T)
    perm = (pos[None, :] == place[:, None]).astype(BF)
    xs = mm(perm, hidden_in)
    dys = mm(perm, out_grad).astype(BF)
    doc = doc_ids[0]
    allowed = (place[None, :] <= place[:, None]) & (doc[:, None] == doc[None, :])
    allowed = mm(mm(perm, allowed.astype(BF)).astype(BF), perm, ((1,), (1,))) > 0.5
    is0 = (place < n0)[:, None]
    small = jnp.stack(
        [
            ln1_gain,
            ln1_bias,
            ln2_gain,
            ln2_bias,
            w_router[:, 0],
            w_router[:, 1],
            w_mix[:, 0],
            w_mix[:, 1],
        ]
    ).astype(F32)
    small = lax.all_gather(small, BOTH, axis=1, tiled=True)
    g1, b1, g2, b2 = (small[0], small[1], small[2], small[3])
    wr, wm = (small[4:6], small[6:8])
    wa = jnp.stack([w_query, w_key, w_value, w_out])
    wa = lax.all_gather(wa, BOTH, axis=1, tiled=True)
    wq, wk, wv, wo = (wa[0], wa[1], wa[2], wa[3])
    ups = jnp.stack([w_up, expert_up[0], expert_up[1]])
    ups = ups.reshape(3, WR, C, S, FR).transpose(3, 0, 1, 2, 4).reshape(S, 3, WR, F)
    ups = lax.all_to_all(ups, "shard", 0, 0)
    ups = lax.all_gather(ups, "dp", axis=0)
    ups = ups.transpose(2, 0, 1, 3, 4).reshape(3, D, F)
    downs = jnp.stack([w_down, expert_down[0], expert_down[1]])
    downs = lax.all_gather(downs, "dp", axis=1, tiled=True)
    dy_all = ag(dys)
    n1, u1, i1 = layer_norm(xs, g1, b1)
    h1b = n1.astype(BF)
    q = (mm(h1b, wq) * 0.125).astype(BF).reshape(T, H, HD)
    k = mm(h1b, wk).astype(BF).reshape(T, H, HD)
    v = mm(h1b, wv).astype(BF).reshape(T, H, HD)
    s = jnp.einsum("ihd,jhd->hij", q, k, preferred_element_type=F32)
    s = jnp.where(allowed[None], s, -1e30)
    ex = jnp.exp(s - jnp.max(s, axis=-1, keepdims=True))
    p = ex / jnp.sum(ex, axis=-1, keepdims=True)
    pb = p.astype(BF)
    o = jnp.einsum("hij,jhd->ihd", pb, v, preferred_element_type=F32).reshape(T, D).astype(BF)
    x1 = xs + mm(o, wo)
    h2, u2, i2 = layer_norm(x1, g2, b2)
    h2b = h2.astype(BF)

    def two(w):
        return jnp.stack([jnp.sum(h2 * w[0], axis=-1), jnp.sum(h2 * w[1], axis=-1)], axis=-1)

    r = jax.nn.softmax(two(wr), axis=-1)
    c = jax.nn.softmax(two(wm), axis=-1)
    gate = jnp.where(is0, r[:, 0:1], r[:, 1:2])
    c0, c1 = (c[:, 0:1], c[:, 1:2])
    we = c0 * gate
    scal = jnp.concatenate([c1, jnp.where(is0, we, 0.0), jnp.where(is0, 0.0, we)], axis=1)
    h_all = ag(h2b)
    scal_all = ag(scal)

    def cut(a, e):
        return (a[:, :LO] if e == 1 else a[:, HI:]) if e else a

    partial_y = jnp.zeros((S, T, D), F32)
    partial_dh = jnp.zeros((S, T, D), F32)
    score = []
    gup, gdown = ([], [])
    for e in range(3):
        he = cut(h_all, e)
        dye = cut(dy_all, e).astype(F32)
        se = cut(scal_all, e)[:, :, e : e + 1]
        n = he.shape[1]
        hf = he.reshape(S * n, D)
        pre = mm(hf, ups[e])
        val, der = gelu_pair(pre)
        ub = val.astype(BF)
        m = mm(ub, downs[e]).reshape(S, n, D)
        dm = (dye * se).astype(BF).reshape(S * n, D)
        dg = (mm(dm, downs[e], ((1,), (1,))) * der).astype(BF)
        gdown.append(mm(ub, dm, ((0,), (0,))))
        gup.append(mm(hf, dg, ((0,), (0,))))
        dx = mm(dg, ups[e], ((1,), (1,))).reshape(S, n, D)
        y = m * se
        sc = jnp.sum(dye * m, axis=-1)
        pad = [(0, 0), (0, T - n) if e < 2 else (T - n, 0)]
        live = is0[None, :, 0]
        partial_y += jnp.pad(y, pad + [(0, 0)])
        partial_dh += jnp.pad(dx, pad + [(0, 0)])
        score.append(jnp.pad(sc, pad))
    yfull = rs(partial_y)
    dh2 = rs(partial_dh)
    sc = lax.psum_scatter(jnp.stack(score, axis=1), "shard", scatter_dimension=0, tiled=False)
    sm = sc[0][:, None]
    se = jnp.where(is0, sc[1][:, None], sc[2][:, None])
    dc0, dc1 = (gate * se, sm)
    tot = c0 * dc0 + c1 * dc1
    dcl0, dcl1 = (c0 * (dc0 - tot), c1 * (dc1 - tot))
    dgate = c0 * se
    dr0, dr1 = (jnp.where(is0, dgate, 0.0), jnp.where(is0, 0.0, dgate))
    tot = r[:, 0:1] * dr0 + r[:, 1:2] * dr1
    drl0, drl1 = (r[:, 0:1] * (dr0 - tot), r[:, 1:2] * (dr1 - tot))
    layer_out = (x1 + yfull).astype(BF)
    dh2 = dh2 + drl0 * wr[0] + drl1 * wr[1] + dcl0 * wm[0] + dcl1 * wm[1]
    gw = [jnp.sum(h2 * t, axis=0) for t in (drl0, drl1, dcl0, dcl1)]
    dx1, gg2, gb2 = norm_back(dh2, u2, i2, g2)
    dx1 = dx1 + dys.astype(F32)
    dab = dx1.astype(BF)
    gwo = mm(o, dab, ((0,), (0,)))
    do = mm(dab, wo, ((1,), (1,))).astype(BF).reshape(T, H, HD)
    dp = jnp.einsum("ihd,jhd->hij", do, v, preferred_element_type=F32)
    ds = (p * (dp - jnp.sum(p * dp, axis=-1, keepdims=True))).astype(BF)
    dq = jnp.einsum("hij,jhd->ihd", ds, k, preferred_element_type=F32).astype(BF)
    dq = (dq * BF(0.125)).reshape(T, D)
    dk = jnp.einsum("hij,ihd->jhd", ds, q, preferred_element_type=F32).astype(BF).reshape(T, D)
    dv = jnp.einsum("hij,ihd->jhd", pb, do, preferred_element_type=F32).astype(BF).reshape(T, D)
    dh1 = mm(dq, wq, ((1,), (1,))) + mm(dk, wk, ((1,), (1,))) + mm(dv, wv, ((1,), (1,)))
    ga = jnp.stack(
        [mm(h1b, dq, ((0,), (0,))), mm(h1b, dk, ((0,), (0,))), mm(h1b, dv, ((0,), (0,))), gwo]
    )
    dxn, gg1, gb1 = norm_back(dh1, u1, i1, g1)
    input_grad = (dx1 + dxn).astype(BF)
    layer_out = mm(perm, layer_out, ((0,), (0,))).astype(BF)
    input_grad = mm(perm, input_grad, ((0,), (0,))).astype(BF)
    smalls = lax.psum(jnp.stack([gg1, gb1, gg2, gb2] + gw), BOTH)
    mine = lax.dynamic_slice_in_dim(smalls, lax.axis_index(BOTH) * WR, WR, 1)
    ga = ga.reshape(4, C, S, WR, D).transpose(1, 2, 0, 3, 4)
    ga = lax.psum_scatter(ga.astype(BF), "dp", scatter_dimension=0, tiled=False)
    ga = lax.psum_scatter(ga, "shard", scatter_dimension=0, tiled=False).astype(F32)
    gdown = lax.psum_scatter(jnp.stack(gdown), "dp", scatter_dimension=1, tiled=True)
    gup = jnp.stack(gup).reshape(3, C, S, WR, F).transpose(1, 2, 0, 3, 4)
    gup = lax.psum_scatter(gup, "dp", scatter_dimension=0, tiled=False).astype(BF)
    gup = lax.all_to_all(gup, "shard", 0, 0).astype(F32)
    gup = gup.reshape(S, 3, WR, C, FR).transpose(1, 2, 3, 0, 4).reshape(3, WR, FF)
    counts = lax.psum(jnp.stack([n0, T - n0]), BOTH)
    load_new = 0.9 * load_avg + 0.1 * counts.astype(F32) * E / (T * C * S)
    return (
        layer_out,
        input_grad,
        mine[0],
        mine[1],
        ga[0],
        ga[1],
        ga[2],
        ga[3],
        mine[2],
        mine[3],
        gup[0],
        gdown[0],
        jnp.stack([mine[4], mine[5]], axis=1),
        jnp.stack([mine[6], mine[7]], axis=1),
        gup[1:],
        gdown[1:],
        counts,
        load_new,
    )


def solution(mesh):
    row, vec = (P(BOTH, None), P(BOTH))
    mid = P(None, BOTH, None)
    return jax.shard_map(
        body,
        mesh=mesh,
        in_specs=(
            row,
            row,
            vec,
            vec,
            row,
            vec,
            vec,
            row,
            row,
            row,
            row,
            vec,
            vec,
            row,
            row,
            row,
            row,
            mid,
            mid,
            P(),
        ),
        out_specs=(
            row,
            row,
            vec,
            vec,
            row,
            row,
            row,
            row,
            vec,
            vec,
            row,
            row,
            row,
            row,
            mid,
            mid,
            P(),
            P(),
        ),
        check_vma=False,
    )
```

profile of v0, /device:TPU:0, one launch (start us, length us, event | category | flops | bytes accessed | tf_op | source)
XLA Modules:
  0.0 906.7 jit_solution(14686394213423674145)
XLA Ops:
  13.6 8.3 all-to-all-start
  22.1 81.6 %all-gather.4 = f32[32,32,8]{1,2,0:T(8,128)S(1)} all-gather(f32[1,32,8]{1,2,0:T(8,128)S(1)} %convert_bitcast_fusion.4), channel_id=1, replica_groups=mesh['dp'=2,'shard'=16] {'dp','shard'}, dimensions={0}, use_global_device_ids=true | all-gather | bytes 33792 | tf_op jit(solution)/shard_map/all_gather | solution.py:105
  107.2 2.1 fusion.40
  109.5 2.2 fusion.42
  111.8 2.4 fusion.41
  116.6 2.1 fusion.118
  125.9 70.1 %all-gather.15.cloned.1.call-done = bf16[2048,1024]{1,0:T(8,128)(2,1)} async-done(((bf16[128,1024]{1,0:T(8,128)(2,1)}), bf16[2048,1024]{1,0:T(8,128)(2,1)}) %all-gather.15.cloned.1.call-update) | async-done | bytes 4194320 | tf_op jit(solution)/shard_map/all_gather | solution.py:42
  196.0 3.2 fusion.113
  199.2 2.8 multiply_convert_fusion.1
  202.1 2.4 multiply_convert_fusion.2
  205.8 4.4 fusion.52
  210.2 76.1 %all-gather.19.cloned.1.call-done = bf16[2048,1024]{1,0:T(8,128)(2,1)} async-done(((bf16[128,1024]{1,0:T(8,128)(2,1)}), bf16[2048,1024]{1,0:T(8,128)(2,1)}) %all-gather.19.cloned.1.call-update) | async-done | bytes 4194320 | tf_op jit(solution)/shard_map/all_gather | solution.py:42
  286.3 8.0 fusion.4
  294.4 2.9 multiply_convert_fusion
  297.4 6.0 fusion.2
  303.4 74.4 %all-reduce.6 = f32[16,3,128]{2,1,0:T(4,128)S(1)} all-reduce(f32[16,3,128]{2,1,0:T(4,128)S(1)} %pad_maximum_fusion.3), channel_id=8, replica_groups=mesh['dp'=2,'shard'=16] {'shard'}, use_global_device_ids=true, to_apply=%region_18.19.clone | all-reduce | flops 6144 | bytes 49152
  380.5 35.8 %all-gather.2 = f32[2048,3]{0,1:T(4,128)S(1)} all-gather(f32[128,3]{0,1:T(4,128)S(1)} %pad_maximum_fusion.4), channel_id=4, replica_groups=mesh['dp'=2,'shard'=16] {'shard'}, dimensions={0}, use_global_device_ids=true | all-gather | bytes 26112 | tf_op jit(solution)/shard_map/all_gather | solution.py:42
  416.4 10.2 %fusion.3 = (bf16[16,80,1024]{2,1,0:T(8,128)(2,1)S(1)}, bf16[16,80,1024]{2,1,0:T(8,128)(2,1)S(1)}, f32[16,80,1024]{2,1,0:T(8,128)}, f32[16,80,1024]{2,1,0:T(8,128)}) fusion(f32[16,80]{1,0:T(8,128)S(1)} %get-tuple-element.62, bf16[16,128,1024]{2,1,0:T(8,128)(2,1)} %bitcast.390, f32[16,80]{1,0:T(8,128)S(1)} %get-tuple-element.63, f32[16,80,1024]{2,1,0:T(8,128)} %fusion.52, ...), kind=kLoop, calls=%fused_computation.12 | loop fusion | flops 10485760 | bytes 31467520 | tf_op jit(solution)/shard_map/convert_element_type | solution.py:163
  428.0 3.2 fusion.119
  432.7 3.5 fusion.120
  436.2 1.9 copy-done.3
  438.2 7.0 fusion.1
  445.2 5.2 fusion.7
  451.4 2.9 add_convert_fusion
  454.9 92.5 %reduce-scatter.15.cloned.1.call-done = bf16[1,128,1024]{2,1,0:T(8,128)(2,1)} async-done(((bf16[16,128,1024]{2,1,0:T(8,128)(2,1)}), bf16[1,128,1024]{2,1,0:T(8,128)(2,1)}) %reduce-scatter.15.cloned.1.call-update) | async-done | bytes 262160 | tf_op jit(solution)/shard_map/reduce_scatter | solution.py:46
  549.4 2.5 fusion.39
  560.0 3.8 maximum_bitcast_fusion
  563.9 3.0 convolution_bitcast_fusion
  570.4 2.0 pad_maximum_fusion
  574.0 4.6 copy.102
  578.7 4.4 copy.103
  583.1 6.6 copy.101
  589.7 3.3 convolution_bitcast_fusion.4
  594.1 2.0 copy-done.8
  597.3 2.0 maximum_bitcast_fusion.1
  599.3 12.2 %all-reduce.17 = bf16[2,16,3,32,256]{4,3,1,0,2:T(8,128)(2,1)S(1)} all-reduce(f32[2,16,3,32,256]{4,3,1,0,2:T(8,128)} %maximum_bitcast_fusion.1), channel_id=11, replica_groups=mesh['dp'=2,'shard'=16] {'dp'}, use_global_device_ids=true, to_apply=%region_35.36.clone | all-reduce | flops 786432 | bytes 4718592
  613.2 5.7 all-to-all-start.1
  619.0 5.6 dynamic-slice_bitcast_fusion
  626.0 48.3 %psum.15 = s32[2]{0:T(128)S(1)} all-reduce(s32[2]{0:T(128)S(1)} %pad_add_fusion), channel_id=1, replica_groups=mesh['dp'=2,'shard'=16] {'dp','shard'}, use_global_device_ids=true, to_apply=%region_37.38 | all-reduce | flops 2 | bytes 16 | tf_op jit(solution)/shard_map/psum | solution.py:219
  674.8 2.0 reshape.306
  680.8 2.3 slice.285
  683.1 1.9 slice_bitcast_fusion.28
  685.0 2.4 fusion.17
  687.5 2.5 fusion.15
  690.0 2.6 multiply_reduce_fusion.6
  692.7 43.1 %psum.14 = f32[8,1024]{1,0:T(8,128)S(1)} all-reduce(f32[8,1024]{1,0:T(8,128)S(1)} %stack.176), channel_id=1, replica_groups=mesh['dp'=2,'shard'=16] {'dp','shard'}, use_global_device_ids=true, to_apply=%region_32.33 | all-reduce | flops 8192 | bytes 65536 | tf_op jit(solution)/shard_map/psum | solution.py:209
  737.6 2.0 convolution_convert_fusion.5
  740.6 156.4 %all-reduce.16.cloned.1.call-done = bf16[16,4,32,1024]{3,2,0,1:T(8,128)(2,1)} async-done(((bf16[16,4,32,1024]{3,2,0,1:T(8,128)(2,1)}), bf16[16,4,32,1024]{3,2,0,1:T(8,128)(2,1)}) %all-reduce.16.cloned.1.call-update) | async-done | bytes 4194320
  (255 shorter events, 57.9 us)
Async XLA Ops:
  7.2 98.4 %copy-start = (bf16[128,1024]{1,0:T(8,128)(2,1)S(1)}, bf16[128,1024]{1,0:T(8,128)(2,1)}, u32[]{:S(2)}) copy-start(bf16[128,1024]{1,0:T(8,128)(2,1)} %param.20) | copy-start | bytes 786436
  7.2 3.5 copy-start.38
  7.2 100.0 %all-gather.11.cloned.1.call-start = ((), (), s32[]{:S(2)}) async-start(), calls=%async_computation.5 | async-start | bytes 8650752 | tf_op jit(solution)/shard_map/all_gather | solution.py:109
  11.0 10.9 %copy-start.44 = (bf16[32,2]{0,1:T(2,128)(2,1)S(1)}, bf16[32,2]{0,1:T(2,128)(2,1)}, u32[]{:S(2)}) copy-start(bf16[32,2]{0,1:T(2,128)(2,1)} %param.36) | copy-start | bytes 388
  11.1 10.9 %copy-start.45 = (bf16[32,2]{0,1:T(2,128)(2,1)S(1)}, bf16[32,2]{0,1:T(2,128)(2,1)}, u32[]{:S(2)}) copy-start(bf16[32,2]{0,1:T(2,128)(2,1)} %param.35) | copy-start | bytes 388
  11.1 10.9 %copy-start.46 = (bf16[32]{0:T(256)(128)(2,1)S(1)}, bf16[32]{0:T(256)(128)(2,1)}, u32[]{:S(2)}) copy-start(bf16[32]{0:T(256)(128)(2,1)} %param.25) | copy-start | bytes 196
  11.1 10.9 %copy-start.47 = (bf16[32]{0:T(256)(128)(2,1)S(1)}, bf16[32]{0:T(256)(128)(2,1)}, u32[]{:S(2)}) copy-start(bf16[32]{0:T(256)(128)(2,1)} %param.26) | copy-start | bytes 196
  11.1 10.9 %copy-start.48 = (bf16[32]{0:T(256)(128)(2,1)S(1)}, bf16[32]{0:T(256)(128)(2,1)}, u32[]{:S(2)}) copy-start(bf16[32]{0:T(256)(128)(2,1)} %param.31) | copy-start | bytes 196
  11.1 10.9 %copy-start.49 = (bf16[32]{0:T(256)(128)(2,1)S(1)}, bf16[32]{0:T(256)(128)(2,1)}, u32[]{:S(2)}) copy-start(bf16[32]{0:T(256)(128)(2,1)} %param.32) | copy-start | bytes 196
  12.1 91.7 %copy-start.51 = (s32[128]{0:T(128)S(1)}, s32[128]{0:T(128)}, u32[]{:S(2)}) copy-start(s32[128]{0:T(128)} %param.22) | copy-start | bytes 1540
  12.2 92.3 %copy-start.50 = (s32[128]{0:T(128)S(1)}, s32[128]{0:T(128)}, u32[]{:S(2)}) copy-start(s32[128]{0:T(128)} %param.23) | copy-start | bytes 1540
  12.2 93.0 %copy-start.52 = (s32[1,128]{1,0:T(1,128)S(1)}, s32[1,128]{1,0:T(1,128)}, u32[]{:S(2)}) copy-start(s32[1,128]{1,0:T(1,128)} %param.21) | copy-start | bytes 1540
  13.6 92.6 %all-to-all-start = ((bf16[16,3,32,256]{3,2,1,0:T(8,128)(2,1)}), bf16[16,3,32,256]{3,2,1,0:T(8,128)(2,1)S(1)}, u32[]{:S(2)}, u32[]{:S(2)}) async-start(bf16[16,3,32,256]{3,2,1,0:T(8,128)(2,1)} %reshape.288), calls=%async_computation | async-start | bytes 1572864 | tf_op jit(solution)/shard_map/all_to_all | solution.py:113
  21.9 101.5 %all-gather.17.cloned.1.call-start = ((), (), s32[]{:S(2)}) async-start(), calls=%async_computation.11 | async-start | bytes 2359296 | tf_op jit(solution)/shard_map/all_gather | solution.py:114
  107.1 88.9 %all-gather.15.cloned.1.call-start = ((), (), s32[]{:S(2)}) async-start(), calls=%async_computation.10 | async-start | bytes 4456448 | tf_op jit(solution)/shard_map/all_gather | solution.py:42
  109.5 6.4 copy-start.26
  111.8 4.0 copy-start.28
  119.3 3.4 copy-start.55
  120.1 85.7 %all-gather.13.cloned.1.call-start = ((), (), s32[]{:S(2)}) async-start(), calls=%async_computation.6 | async-start | bytes 2359296 | tf_op jit(solution)/shard_map/all_gather | solution.py:117
  121.2 165.1 %all-gather.19.cloned.1.call-start = ((), (), s32[]{:S(2)}) async-start(), calls=%async_computation.12 | async-start | bytes 4456448 | tf_op jit(solution)/shard_map/all_gather | solution.py:42
  122.2 425.2 %reduce-scatter.15.cloned.1.call-start = ((), (), s32[]{:S(2)}) async-start(), calls=%async_computation.8 | async-start | bytes 4456448 | tf_op jit(solution)/shard_map/reduce_scatter | solution.py:46
  286.3 8.1 copy-start.4
  297.4 6.0 copy-start.21
  416.4 10.2 %copy-start.20 = (bf16[3,256,1024]{2,1,0:T(8,128)(2,1)S(1)}, bf16[3,256,1024]{2,1,0:T(8,128)(2,1)}, u32[]{:S(2)}) copy-start(bf16[3,256,1024]{2,1,0:T(8,128)(2,1)} %all-gather.13.cloned.1.call-done) | copy-start | bytes 4718596
  416.4 10.2 %copy-start.58 = (f32[1280,256]{1,0:T(8,128)S(1)}, f32[1280,256]{1,0:T(8,128)}, u32[]{:S(2)}) copy-start(f32[1280,256]{1,0:T(8,128)} %get-tuple-element.97) | copy-start | bytes 3932164
  426.5 4.7 copy-start.12
  431.2 5.0 slice-start
  431.2 5.0 slice-start.1
  432.7 3.6 copy-start.34
  432.7 5.5 copy-start.3
  445.1 6.2 slice-start.2
  445.1 6.2 slice-start.4
  445.1 6.2 slice-start.3
  445.1 6.2 slice-start.5
  454.3 94.8 %copy-start.14 = (bf16[128,1024]{1,0:T(8,128)(2,1)S(1)}, bf16[128,1024]{1,0:T(8,128)(2,1)}, u32[]{:S(2)}) copy-start(bf16[128,1024]{1,0:T(8,128)(2,1)} %convolution_convert_fusion.4) | copy-start | bytes 786436
  454.3 164.6 %all-reduce.14.cloned.1.call-start = ((), (), s32[]{:S(2)}) async-start(), calls=%async_computation.13 | async-start | bytes 16777216
  563.9 116.9 %reduce-scatter.17.cloned.1.call-start = ((), (), s32[]{:S(2)}) async-start(), calls=%async_computation.9 | async-start | bytes 4718592 | tf_op jit(solution)/shard_map/reduce_scatter | solution.py:214
  563.9 3.9 copy-start.22
  572.5 165.1 %reduce-scatter.13.cloned.1.call-start = ((), (), s32[]{:S(2)}) async-start(), calls=%async_computation.7 | async-start | bytes 4456448 | tf_op jit(solution)/shard_map/reduce_scatter | solution.py:46
  589.7 3.3 copy-start.13
  589.7 3.5 copy-start.35
  589.7 4.4 copy-start.24
  613.2 61.6 %all-to-all-start.1 = ((bf16[16,3,32,256]{3,2,1,0:T(8,128)(2,1)}), bf16[16,3,32,256]{3,2,1,0:T(8,128)(2,1)}, u32[]{:S(2)}, u32[]{:S(2)}) async-start(bf16[16,3,32,256]{3,2,1,0:T(8,128)(2,1)} %copy.104), calls=%async_computation.3 | async-start | bytes 1572864 | tf_op jit(solution)/shard_map/all_to_all | solution.py:217
  618.9 278.1 %all-reduce.16.cloned.1.call-start = ((), (), s32[]{:S(2)}) async-start(), calls=%async_computation.14 | async-start | bytes 8388608
  624.6 49.7 %copy-start.53 = (f32[2]{0:T(128)S(1)}, f32[2]{0:T(128)}, u32[]{:S(2)}) copy-start(f32[2]{0:T(128)} %param.39) | copy-start | bytes 28
  679.9 5.2 copy-start.31
  683.1 4.4 copy-start.43
  737.6 161.9 %copy-start.1 = (bf16[128,1024]{1,0:T(8,128)(2,1)S(1)}, bf16[128,1024]{1,0:T(8,128)(2,1)}, u32[]{:S(2)}) copy-start(bf16[128,1024]{1,0:T(8,128)(2,1)} %param.20) | copy-start | bytes 786436
  (29 other events, 60.4 us)
Sparse Core Ops, SparseCore 0:
  11.5 86.9 all-gather.10
  107.2 8.1 all-gather.16
  120.2 75.7 all-gather.14
  197.4 8.3 all-gather.12
  209.0 77.2 all-gather.18
  454.4 92.9 reduce-scatter.14
  564.0 38.4 all-reduce.13
  604.7 12.2 reduce-scatter.16
  619.4 101.9 reduce-scatter.12
  727.8 169.1 all-reduce.15
where the time goes:
time: 914 us; the launch traced here: 907 us
  waiting for transfers between devices  397 us (43%)
  blocking collectives  296 us (32%)
  matrix products  86.9 us (10%)
  local copies, waits for them, and re-layouts  55.6 us (6%)
  other arithmetic  40 us (4%)
  between operations  16.4 us (2%)
  starting transfers between devices  15.4 us (2%)
    unnamed x12, waiting for transfers between devices  157 us
    all_gather x2, waiting for transfers between devices, ag(): return lax.all_gather(block, 'shard', axis=0, tiled=False)  146 us
    reduce_scatter x2, waiting for transfers between devices, rs(): lax.psum_scatter(parts.astype(BF), 'shard', scatter_dimension=0, tiled=Fa...  92.5 us
    unnamed x2, blocking collectives  86.7 us
    all_gather x1, blocking collectives, body(): small = lax.all_gather(small, BOTH, axis=1, tiled=True)  81.6 us
    dot_general x35, matrix products, mm(): return lax.dot_general(a, b, (dims, ((), ())), preferred_element_type=F32)  80.9 us
    psum x1, blocking collectives, body(): counts = lax.psum(jnp.stack([n0, T - n0]), BOTH)  48.3 us
    psum x1, blocking collectives, body(): smalls = lax.psum(jnp.stack([gg1, gb1, gg2, gb2] + gw), BOTH)  43.1 us
  transfers between devices with their start and end apart: 12, of which 5 were waited for; matrix products, arithmetic and copies ran while one was open for 11% of the time, Pallas kernels for 0%

commit v1 on v0

--- a/solution.py
+++ b/solution.py
@@ -8,6 +8,12 @@
 BF = jnp.bfloat16
 F32 = jnp.float32
 BOTH = ("dp", "shard")
+
+
+def gather_and_add(x, axis):
+    parts = lax.all_gather(x, axis, axis=0, tiled=False)
+    total = parts.sum(axis=0)
+    return total
 
 
 def mm(a, b, dims=((1,), (0,))):
@@ -216,7 +222,7 @@
     gup = lax.psum_scatter(gup, "dp", scatter_dimension=0, tiled=False).astype(BF)
     gup = lax.all_to_all(gup, "shard", 0, 0).astype(F32)
     gup = gup.reshape(S, 3, WR, C, FR).transpose(1, 2, 3, 0, 4).reshape(3, WR, FF)
-    counts = lax.psum(jnp.stack([n0, T - n0]), BOTH)
+    counts = gather_and_add(jnp.stack([n0, T - n0]), BOTH)
     load_new = 0.9 * load_avg + 0.1 * counts.astype(F32) * E / (T * C * S)
     return (
         layer_out,

time: 914 us -> 914 us (level)
    psum x1 -> x0, blocking collectives: 48.3 us -> none  [body(): counts = lax.psum(jnp.stack([n0, T - n0]), BOTH)]
    unnamed x2 -> x3, blocking collectives: 86.7 us -> 135 us
where the time goes in v1:
time: 914 us; the launch traced here: 907 us
  waiting for transfers between devices  397 us (43%)
  blocking collectives  296 us (32%)
  matrix products  86.9 us (10%)
  local copies, waits for them, and re-layouts  55.5 us (6%)
  other arithmetic  40.1 us (4%)
  between operations  16.5 us (2%)
  starting transfers between devices  15.5 us (2%)
    unnamed x12, waiting for transfers between devices  156 us
    all_gather x2, waiting for transfers between devices, ag(): return lax.all_gather(block, 'shard', axis=0, tiled=False)  146 us
    unnamed x3, blocking collectives  135 us
    reduce_scatter x2, waiting for transfers between devices, rs(): lax.psum_scatter(parts.astype(BF), 'shard', scatter_dimension=0, tiled=Fa...  92.5 us
    all_gather x1, blocking collectives, body(): small = lax.all_gather(small, BOTH, axis=1, tiled=True)  81.6 us
    dot_general x35, matrix products, mm(): return lax.dot_general(a, b, (dims, ((), ())), preferred_element_type=F32)  80.9 us
    psum x1, blocking collectives, body(): smalls = lax.psum(jnp.stack([gg1, gb1, gg2, gb2] + gw), BOTH)  43.5 us
    all_gather x1, blocking collectives, ag(): return lax.all_gather(block, 'shard', axis=0, tiled=False)  35.8 us
  transfers between devices with their start and end apart: 12, of which 5 were waited for; matrix products, arithmetic and copies ran while one was open for 11% of the time, Pallas kernels for 0%

profile of v1, /device:TPU:0, one launch (start us, length us, event | category | flops | bytes accessed | tf_op | source)
XLA Modules:
  0.0 906.8 jit_solution(3433247173874429231)
XLA Ops:
  13.6 8.3 all-to-all-start
  22.1 81.6 %all-gather.5 = f32[32,32,8]{1,2,0:T(8,128)S(1)} all-gather(f32[1,32,8]{1,2,0:T(8,128)S(1)} %convert_bitcast_fusion.4), channel_id=1, replica_groups=mesh['dp'=2,'shard'=16] {'dp','shard'}, dimensions={0}, use_global_device_ids=true | all-gather | bytes 33792 | tf_op jit(solution)/shard_map/all_gather | solution.py:111
  107.2 2.1 fusion.40
  109.5 2.2 fusion.42
  111.8 2.4 fusion.41
  116.6 2.1 fusion.118
  125.9 70.1 %all-gather.16.cloned.1.call-done = bf16[2048,1024]{1,0:T(8,128)(2,1)} async-done(((bf16[128,1024]{1,0:T(8,128)(2,1)}), bf16[2048,1024]{1,0:T(8,128)(2,1)}) %all-gather.16.cloned.1.call-update) | async-done | bytes 4194320 | tf_op jit(solution)/shard_map/all_gather | solution.py:48
  196.0 3.2 fusion.113
  199.2 2.8 multiply_convert_fusion.1
  202.1 2.3 multiply_convert_fusion.2
  205.8 4.4 fusion.52
  210.2 76.1 %all-gather.20.cloned.1.call-done = bf16[2048,1024]{1,0:T(8,128)(2,1)} async-done(((bf16[128,1024]{1,0:T(8,128)(2,1)}), bf16[2048,1024]{1,0:T(8,128)(2,1)}) %all-gather.20.cloned.1.call-update) | async-done | bytes 4194320 | tf_op jit(solution)/shard_map/all_gather | solution.py:48
  286.3 8.0 fusion.4
  294.4 2.9 multiply_convert_fusion
  297.4 6.0 fusion.2
  303.4 74.4 %all-reduce.7 = f32[16,3,128]{2,1,0:T(4,128)S(1)} all-reduce(f32[16,3,128]{2,1,0:T(4,128)S(1)} %pad_maximum_fusion.3), channel_id=9, replica_groups=mesh['dp'=2,'shard'=16] {'shard'}, use_global_device_ids=true, to_apply=%region_18.19.clone | all-reduce | flops 6144 | bytes 49152
  380.5 35.8 %all-gather.2 = f32[2048,3]{0,1:T(4,128)S(1)} all-gather(f32[128,3]{0,1:T(4,128)S(1)} %pad_maximum_fusion.4), channel_id=4, replica_groups=mesh['dp'=2,'shard'=16] {'shard'}, dimensions={0}, use_global_device_ids=true | all-gather | bytes 26112 | tf_op jit(solution)/shard_map/all_gather | solution.py:48
  416.4 10.2 %fusion.3 = (bf16[16,80,1024]{2,1,0:T(8,128)(2,1)S(1)}, bf16[16,80,1024]{2,1,0:T(8,128)(2,1)S(1)}, f32[16,80,1024]{2,1,0:T(8,128)}, f32[16,80,1024]{2,1,0:T(8,128)}) fusion(f32[16,80]{1,0:T(8,128)S(1)} %get-tuple-element.62, bf16[16,128,1024]{2,1,0:T(8,128)(2,1)} %bitcast.390, f32[16,80]{1,0:T(8,128)S(1)} %get-tuple-element.63, f32[16,80,1024]{2,1,0:T(8,128)} %fusion.52, ...), kind=kLoop, calls=%fused_computation.12 | loop fusion | flops 10485760 | bytes 31467520 | tf_op jit(solution)/shard_map/convert_element_type | solution.py:169
  428.1 3.2 fusion.119
  432.7 3.5 fusion.120
  436.3 1.9 copy-done.3
  438.2 7.0 fusion.1
  445.2 5.2 fusion.7
  451.4 2.9 add_convert_fusion
  455.0 92.5 %reduce-scatter.15.cloned.1.call-done = bf16[1,128,1024]{2,1,0:T(8,128)(2,1)} async-done(((bf16[16,128,1024]{2,1,0:T(8,128)(2,1)}), bf16[1,128,1024]{2,1,0:T(8,128)(2,1)}) %reduce-scatter.15.cloned.1.call-update) | async-done | bytes 262160 | tf_op jit(solution)/shard_map/reduce_scatter | solution.py:52
  549.4 2.5 fusion.39
  560.1 3.8 maximum_bitcast_fusion
  564.0 3.0 convolution_bitcast_fusion
  570.5 2.1 pad_maximum_fusion
  574.1 4.6 copy.102
  578.7 4.4 copy.103
  583.1 6.5 copy.101
  589.7 3.3 convolution_bitcast_fusion.4
  594.0 1.9 copy-done.8
  597.2 2.0 maximum_bitcast_fusion.1
  599.2 12.2 %all-reduce.18 = bf16[2,16,3,32,256]{4,3,1,0,2:T(8,128)(2,1)S(1)} all-reduce(f32[2,16,3,32,256]{4,3,1,0,2:T(8,128)} %maximum_bitcast_fusion.1), channel_id=12, replica_groups=mesh['dp'=2,'shard'=16] {'dp'}, use_global_device_ids=true, to_apply=%region_35.36.clone | all-reduce | flops 786432 | bytes 4718592
  613.1 5.8 all-to-all-start.1
  619.0 5.6 dynamic-slice_bitcast_fusion
  626.1 48.2 %all-reduce.6 = s32[64]{0:T(128)S(1)} all-reduce(s32[64]{0:T(128)S(1)} %add_dynamic-update-slice_fusion), channel_id=6, replica_groups=mesh['dp'=2,'shard'=16] {'dp','shard'}, use_global_device_ids=true, to_apply=%add.6 | all-reduce | flops 64 | bytes 512
  675.0 2.0 reshape.306
  681.0 2.3 slice.285
  683.3 1.9 slice_bitcast_fusion.28
  685.2 2.4 fusion.17
  687.7 2.5 fusion.15
  690.2 2.6 multiply_reduce_fusion.6
  692.8 43.5 %psum.7 = f32[8,1024]{1,0:T(8,128)S(1)} all-reduce(f32[8,1024]{1,0:T(8,128)S(1)} %stack.176), channel_id=1, replica_groups=mesh['dp'=2,'shard'=16] {'dp','shard'}, use_global_device_ids=true, to_apply=%region_32.33 | all-reduce | flops 8192 | bytes 65536 | tf_op jit(solution)/shard_map/psum | solution.py:215
  738.1 2.0 convolution_convert_fusion.5
  741.2 155.9 %all-reduce.17.cloned.1.call-done = bf16[16,4,32,1024]{3,2,0,1:T(8,128)(2,1)} async-done(((bf16[16,4,32,1024]{3,2,0,1:T(8,128)(2,1)}), bf16[16,4,32,1024]{3,2,0,1:T(8,128)(2,1)}) %all-reduce.17.cloned.1.call-update) | async-done | bytes 4194320
  (258 shorter events, 58.1 us)
Async XLA Ops:
  7.2 98.4 %copy-start = (bf16[128,1024]{1,0:T(8,128)(2,1)S(1)}, bf16[128,1024]{1,0:T(8,128)(2,1)}, u32[]{:S(2)}) copy-start(bf16[128,1024]{1,0:T(8,128)(2,1)} %param.20) | copy-start | bytes 786436
  7.2 3.5 copy-start.38
  7.2 100.0 %all-gather.12.cloned.1.call-start = ((), (), s32[]{:S(2)}) async-start(), calls=%async_computation.5 | async-start | bytes 8650752 | tf_op jit(solution)/shard_map/all_gather | solution.py:115
  11.0 10.9 %copy-start.44 = (bf16[32,2]{0,1:T(2,128)(2,1)S(1)}, bf16[32,2]{0,1:T(2,128)(2,1)}, u32[]{:S(2)}) copy-start(bf16[32,2]{0,1:T(2,128)(2,1)} %param.36) | copy-start | bytes 388
  11.1 10.9 %copy-start.45 = (bf16[32,2]{0,1:T(2,128)(2,1)S(1)}, bf16[32,2]{0,1:T(2,128)(2,1)}, u32[]{:S(2)}) copy-start(bf16[32,2]{0,1:T(2,128)(2,1)} %param.35) | copy-start | bytes 388
  11.1 10.9 %copy-start.46 = (bf16[32]{0:T(256)(128)(2,1)S(1)}, bf16[32]{0:T(256)(128)(2,1)}, u32[]{:S(2)}) copy-start(bf16[32]{0:T(256)(128)(2,1)} %param.25) | copy-start | bytes 196
  11.1 10.9 %copy-start.47 = (bf16[32]{0:T(256)(128)(2,1)S(1)}, bf16[32]{0:T(256)(128)(2,1)}, u32[]{:S(2)}) copy-start(bf16[32]{0:T(256)(128)(2,1)} %param.26) | copy-start | bytes 196
  11.1 10.9 %copy-start.48 = (bf16[32]{0:T(256)(128)(2,1)S(1)}, bf16[32]{0:T(256)(128)(2,1)}, u32[]{:S(2)}) copy-start(bf16[32]{0:T(256)(128)(2,1)} %param.31) | copy-start | bytes 196
  11.1 10.9 %copy-start.49 = (bf16[32]{0:T(256)(128)(2,1)S(1)}, bf16[32]{0:T(256)(128)(2,1)}, u32[]{:S(2)}) copy-start(bf16[32]{0:T(256)(128)(2,1)} %param.32) | copy-start | bytes 196
  12.1 91.7 %copy-start.52 = (s32[128]{0:T(128)S(1)}, s32[128]{0:T(128)}, u32[]{:S(2)}) copy-start(s32[128]{0:T(128)} %param.22) | copy-start | bytes 1540
  12.2 92.3 %copy-start.51 = (s32[128]{0:T(128)S(1)}, s32[128]{0:T(128)}, u32[]{:S(2)}) copy-start(s32[128]{0:T(128)} %param.23) | copy-start | bytes 1540
  12.2 93.0 %copy-start.53 = (s32[1,128]{1,0:T(1,128)S(1)}, s32[1,128]{1,0:T(1,128)}, u32[]{:S(2)}) copy-start(s32[1,128]{1,0:T(1,128)} %param.21) | copy-start | bytes 1540
  13.6 92.6 %all-to-all-start = ((bf16[16,3,32,256]{3,2,1,0:T(8,128)(2,1)}), bf16[16,3,32,256]{3,2,1,0:T(8,128)(2,1)S(1)}, u32[]{:S(2)}, u32[]{:S(2)}) async-start(bf16[16,3,32,256]{3,2,1,0:T(8,128)(2,1)} %reshape.288), calls=%async_computation | async-start | bytes 1572864 | tf_op jit(solution)/shard_map/all_to_all | solution.py:119
  21.9 101.5 %all-gather.18.cloned.1.call-start = ((), (), s32[]{:S(2)}) async-start(), calls=%async_computation.11 | async-start | bytes 2359296 | tf_op jit(solution)/shard_map/all_gather | solution.py:120
  107.1 88.9 %all-gather.16.cloned.1.call-start = ((), (), s32[]{:S(2)}) async-start(), calls=%async_computation.10 | async-start | bytes 4456448 | tf_op jit(solution)/shard_map/all_gather | solution.py:48
  109.5 6.4 copy-start.26
  111.8 4.0 copy-start.28
  119.3 3.4 copy-start.56
  120.1 85.7 %all-gather.14.cloned.1.call-start = ((), (), s32[]{:S(2)}) async-start(), calls=%async_computation.6 | async-start | bytes 2359296 | tf_op jit(solution)/shard_map/all_gather | solution.py:123
  121.2 165.1 %all-gather.20.cloned.1.call-start = ((), (), s32[]{:S(2)}) async-start(), calls=%async_computation.12 | async-start | bytes 4456448 | tf_op jit(solution)/shard_map/all_gather | solution.py:48
  122.2 425.2 %reduce-scatter.15.cloned.1.call-start = ((), (), s32[]{:S(2)}) async-start(), calls=%async_computation.8 | async-start | bytes 4456448 | tf_op jit(solution)/shard_map/reduce_scatter | solution.py:52
  286.3 8.1 copy-start.4
  297.4 6.0 copy-start.21
  416.4 10.2 %copy-start.20 = (bf16[3,256,1024]{2,1,0:T(8,128)(2,1)S(1)}, bf16[3,256,1024]{2,1,0:T(8,128)(2,1)}, u32[]{:S(2)}) copy-start(bf16[3,256,1024]{2,1,0:T(8,128)(2,1)} %all-gather.14.cloned.1.call-done) | copy-start | bytes 4718596
  416.4 10.2 %copy-start.58 = (f32[1280,256]{1,0:T(8,128)S(1)}, f32[1280,256]{1,0:T(8,128)}, u32[]{:S(2)}) copy-start(f32[1280,256]{1,0:T(8,128)} %get-tuple-element.97) | copy-start | bytes 3932164
  426.6 4.7 copy-start.12
  431.3 5.0 slice-start
  431.3 5.0 slice-start.1
  432.7 3.6 copy-start.34
  432.7 5.5 copy-start.3
  445.2 6.2 slice-start.2
  445.2 6.2 slice-start.4
  445.2 6.2 slice-start.3
  445.2 6.2 slice-start.5
  454.4 94.8 %copy-start.14 = (bf16[128,1024]{1,0:T(8,128)(2,1)S(1)}, bf16[128,1024]{1,0:T(8,128)(2,1)}, u32[]{:S(2)}) copy-start(bf16[128,1024]{1,0:T(8,128)(2,1)} %convolution_convert_fusion.4) | copy-start | bytes 786436
  454.4 164.6 %all-reduce.15.cloned.1.call-start = ((), (), s32[]{:S(2)}) async-start(), calls=%async_computation.13 | async-start | bytes 16777216
  563.9 117.1 %reduce-scatter.17.cloned.1.call-start = ((), (), s32[]{:S(2)}) async-start(), calls=%async_computation.9 | async-start | bytes 4718592 | tf_op jit(solution)/shard_map/reduce_scatter | solution.py:220
  564.0 3.9 copy-start.22
  572.6 165.5 %reduce-scatter.13.cloned.1.call-start = ((), (), s32[]{:S(2)}) async-start(), calls=%async_computation.7 | async-start | bytes 4456448 | tf_op jit(solution)/shard_map/reduce_scatter | solution.py:52
  589.7 3.3 copy-start.13
  589.7 3.5 copy-start.35
  589.7 4.4 copy-start.24
  613.1 61.9 %all-to-all-start.1 = ((bf16[16,3,32,256]{3,2,1,0:T(8,128)(2,1)}), bf16[16,3,32,256]{3,2,1,0:T(8,128)(2,1)}, u32[]{:S(2)}, u32[]{:S(2)}) async-start(bf16[16,3,32,256]{3,2,1,0:T(8,128)(2,1)} %copy.104), calls=%async_computation.3 | async-start | bytes 1572864 | tf_op jit(solution)/shard_map/all_to_all | solution.py:223
  618.9 278.1 %all-reduce.17.cloned.1.call-start = ((), (), s32[]{:S(2)}) async-start(), calls=%async_computation.14 | async-start | bytes 8388608
  624.6 49.9 %copy-start.54 = (f32[2]{0:T(128)S(1)}, f32[2]{0:T(128)}, u32[]{:S(2)}) copy-start(f32[2]{0:T(128)} %param.39) | copy-start | bytes 28
  680.1 5.2 copy-start.31
  683.3 4.4 copy-start.43
  738.1 161.4 %copy-start.1 = (bf16[128,1024]{1,0:T(8,128)(2,1)S(1)}, bf16[128,1024]{1,0:T(8,128)(2,1)}, u32[]{:S(2)}) copy-start(bf16[128,1024]{1,0:T(8,128)(2,1)} %param.20) | copy-start | bytes 786436
  (29 other events, 60.3 us)
Sparse Core Ops, SparseCore 0:
  11.5 86.9 all-gather.11
  107.2 8.1 all-gather.17
  120.2 75.7 all-gather.15
  197.4 8.3 all-gather.13
  209.0 77.2 all-gather.19
  454.5 92.9 reduce-scatter.14
  564.0 38.4 all-reduce.14
  604.7 12.2 reduce-scatter.16
  619.5 101.9 reduce-scatter.12
  727.9 169.1 all-reduce.16
